TPU v7x, 256 devices: a whole 4x4x8 slice. The times are simulated.
256 devices in a mesh: seq: 32 (over z, x), heads: 8 (over y, core).
Axes of the slice: x: 4, y: 4, z: 8, core: 2. Of those that a mesh axis runs over, the one named last changes fastest.
Arguments:
- lin_q: bfloat16 [8192, 8192], P('seq', 'heads'), may hold values from -4 to 4
- lin_k: bfloat16 [8192, 8192], P('seq', 'heads'), may hold values from -4 to 4
- lin_v: bfloat16 [8192, 8192], P('seq', 'heads'), may hold values from -6 to 6
- decay_rates: float32 [64], P('heads'), may hold values from 3.0517578e-05 to 0.03125
- norm_gain: float32 [8192], P('heads'), may hold values from 0.25 to 1.75
- soft_q: bfloat16 [8192, 8192], P('seq', 'heads'), may hold values from -8 to 8
- soft_k: bfloat16 [8192, 1024], P('seq', 'heads'), may hold values from -8 to 8
- soft_v: bfloat16 [8192, 1024], P('seq', 'heads'), may hold values from -6 to 6
- segment_ids: int32 [8192], P('seq'), may hold values from 0 to 3, never falling along the last dimension, each value on 1 to 6144 neighbouring positions
Outputs:
- lin_out: bfloat16 [8192, 8192], P('seq', 'heads')
- soft_out: bfloat16 [8192, 8192], P('seq', 'heads')
Inputs may be any that keep to these rules, and one draw needn't show every extreme that they name: `segment_ids`: never falling along the sequence; each document has 1 to 6144 tokens, one exactly that many.
All inputs are finite; a program needn't handle non-finite values.
Results may differ from a plain program's by a relative error of at most 0.0049.
Values may be sent and summed in bfloat16 or wider, within the bound.
A program may use at most 128 MiB of HBM per device.

v0:
```python
from functools import partial
import math
import jax
import jax.numpy as jnp
from jax import lax
from jax.sharding import PartitionSpec as P

BLOCK = 256


def carried_in(part, axis, combine, identity):
    place = lax.axis_index(axis)
    gathered = jax.tree.map(lambda a: lax.all_gather(a, axis), part)
    state = jax.tree.map(lambda a, e: jnp.zeros_like(a) + jnp.asarray(e, a.dtype), part, identity)

    def carried_one(step, state):
        return combine(
            state, jax.tree.map(lambda a: lax.dynamic_index_in_dim(a, step, 0, False), gathered)
        )

    return lax.fori_loop(0, place, carried_one, state)


def light_block(carry, inputs, rates):
    state, last_prev = carry
    q_blk, k_blk, v_blk, seg_blk = inputs
    size = q_blk.shape[0]
    seg_f = seg_blk.astype(jnp.float32)
    pos = jnp.arange(size).astype(jnp.float32)
    diff = pos[:, None] - pos[None, :]
    linked = (diff >= 0.0) & (seg_f[:, None] == seg_f[None, :])
    decay = jnp.exp(-rates[:, None, None] * jnp.maximum(diff, 0.0)[None])
    scores = jnp.einsum("thd,shd->hts", q_blk, k_blk, preferred_element_type=jnp.float32)
    weights = jnp.where(linked[None], scores * decay, 0.0).astype(jnp.bfloat16)
    intra = jnp.einsum("hts,shd->thd", weights, v_blk, preferred_element_type=jnp.float32)
    use = (seg_f == last_prev).astype(jnp.float32)
    coef = jnp.exp(-rates[None, :] * (pos[:, None] + 1.0)) * use[:, None]
    q_state = jnp.einsum(
        "thd,hde->the", q_blk.astype(jnp.float32), state, precision=lax.Precision.HIGHEST
    )
    out = intra + coef[:, :, None] * q_state
    last = seg_f[-1]
    k_weight = (
        jnp.exp(-rates[None, :] * (size - 1.0 - pos[:, None]))
        * (seg_f == last).astype(jnp.float32)[:, None]
    )
    k_dec = (k_blk.astype(jnp.float32) * k_weight[:, :, None]).astype(jnp.bfloat16)
    local = jnp.einsum("shd,she->hde", k_dec, v_blk, preferred_element_type=jnp.float32)
    keep = jnp.where(last == last_prev, 1.0, 0.0) * jnp.exp(-rates * size)
    return ((keep[:, None, None] * state + local, last), out)


def combine_states(earlier, later):
    state_e, dec_e, last_e = earlier
    state_l, dec_l, last_l = later
    match = (last_e == last_l) | (last_l < 0.0)
    factor = jnp.where(match, dec_l, 0.0)
    return (factor[:, None, None] * state_e + state_l, dec_e * dec_l, jnp.maximum(last_e, last_l))


def block_update(inner, queries, qpos, seg_rows, k_blk, v_blk, s_blk, kpos, scale):
    mx, den, acc = inner
    shared_heads = k_blk.shape[1]
    group = queries.shape[2]
    query_count = queries.shape[0]
    key_count = k_blk.shape[0]
    heads = shared_heads * group
    s = (
        jnp.einsum("tgjd,sgd->gjts", queries, k_blk, preferred_element_type=jnp.float32).reshape(
            heads, query_count, key_count
        )
        * scale
    )
    mask = (kpos[None, :] <= qpos[:, None]) & (s_blk[None, :] == seg_rows[:, None])
    top = jnp.max(jnp.where(mask[None], s, -1e30), axis=2)
    new_mx = jnp.maximum(mx, top)
    corr = jnp.exp(mx - new_mx)
    p = jnp.where(mask[None], jnp.exp(s - new_mx[:, :, None]), 0.0)
    den = den * corr + jnp.sum(p, axis=2)
    weights = p.astype(jnp.bfloat16).reshape(shared_heads, group, query_count, key_count)
    mixed = jnp.einsum(
        "gjts,sgd->gjtd", weights, v_blk, preferred_element_type=jnp.float32
    ).reshape(heads, query_count, -1)
    acc = acc * corr[:, :, None] + mixed
    return (new_mx, den, acc)


def body(lin_q, lin_k, lin_v, decay_rates, norm_gain, soft_q, soft_k, soft_v, segment_ids):
    tok = lin_q.shape[0]
    heads = decay_rates.shape[0]
    width = lin_q.shape[1] // heads
    blocks = tok // BLOCK
    shape4 = (blocks, BLOCK, heads, width)
    init = (jnp.zeros((heads, width, width), jnp.float32), jnp.float32(-1.0))
    step_fn = lambda c, x: light_block(c, x, decay_rates)
    (state_loc, last_loc), outs = lax.scan(
        step_fn,
        init,
        (
            lin_q.reshape(shape4),
            lin_k.reshape(shape4),
            lin_v.reshape(shape4),
            segment_ids.reshape(blocks, BLOCK),
        ),
    )
    local_out = outs.reshape(tok, heads, width)
    summary = (state_loc, jnp.exp(-decay_rates * tok), last_loc.reshape(1))
    identity = (
        jnp.zeros((heads, width, width), jnp.float32),
        jnp.ones((heads,), jnp.float32),
        jnp.full((1,), -1.0, jnp.float32),
    )
    state_in, dec_in, last_in = carried_in(summary, "seq", combine_states, identity)
    seg_f = segment_ids.astype(jnp.float32)
    pos = jnp.arange(tok).astype(jnp.float32)
    coef = (
        jnp.exp(-decay_rates[None, :] * (pos[:, None] + 1.0))
        * (seg_f == last_in[0]).astype(jnp.float32)[:, None]
    )
    q_three = lin_q.reshape(tok, heads, width)
    q_state = jnp.einsum(
        "thd,hde->the", q_three.astype(jnp.float32), state_in, precision=lax.Precision.HIGHEST
    )
    raw = (local_out + coef[:, :, None] * q_state).reshape(tok, heads * width)
    sums = jnp.sum(raw * raw, axis=1)
    total_sq = lax.psum(sums, "heads")
    count = lax.axis_size("heads") * heads * width
    lin_out = (raw * lax.rsqrt(total_sq / count + 1e-06)[:, None] * norm_gain[None, :]).astype(
        jnp.bfloat16
    )
    scale = 1.0 / math.sqrt(width)
    shared_heads = soft_k.shape[1] // width
    group = heads // shared_heads
    mine = lax.axis_index("seq")
    plans = (soft_q, segment_ids, mine * tok)
    query_sets = []
    query_rows, seg_rows, first = plans
    count_rows = query_rows.shape[0]
    query_sets.append(
        (
            query_rows.reshape(count_rows, shared_heads, group, width),
            first + jnp.arange(count_rows),
            seg_rows,
            first + count_rows - 1,
        )
    )
    start_carry = tuple(
        (
            (
                jnp.full((heads, qs[0].shape[0]), -1e30, jnp.float32),
                jnp.zeros((heads, qs[0].shape[0]), jnp.float32),
                jnp.zeros((heads, qs[0].shape[0], width), jnp.float32),
            )
            for qs in query_sets
        )
    )
    carry = start_carry
    keys = lax.all_gather(soft_k, "seq", axis=0, tiled=True)
    values = lax.all_gather(soft_v, "seq", axis=0, tiled=True)
    seg_keys = lax.all_gather(segment_ids, "seq", axis=0, tiled=True)
    length = keys.shape[0]
    rows = math.gcd(length, 1024)
    count_blk = length // rows
    k_blocks = keys.reshape(count_blk, rows, shared_heads, width)
    v_blocks = values.reshape(count_blk, rows, shared_heads, width)
    s_blocks = seg_keys.reshape(count_blk, rows)

    def attend_one(state, item):
        k_blk, v_blk, s_blk, index = item
        blk_start = index * rows
        kpos = blk_start + jnp.arange(rows)
        fresh = []
        for query_set, inner in zip(query_sets, state):
            queries, qpos, seg_rows, last_pos = query_set
            update = partial(
                block_update,
                queries=queries,
                qpos=qpos,
                seg_rows=seg_rows,
                k_blk=k_blk,
                v_blk=v_blk,
                s_blk=s_blk,
                kpos=kpos,
                scale=scale,
            )
            inner = update(inner)
            fresh.append(inner)
        return (tuple(fresh), None)

    carry, _ = lax.scan(attend_one, carry, (k_blocks, v_blocks, s_blocks, jnp.arange(count_blk)))
    outputs = []
    for mx, den, acc in carry:
        outputs.append(
            (acc / den[:, :, None])
            .transpose(1, 0, 2)
            .reshape(acc.shape[1], heads * width)
            .astype(jnp.bfloat16)
        )
    soft_out = outputs[0]
    return (lin_out, soft_out)


def solution(mesh):
    placed = (
        P("seq", "heads"),
        P("seq", "heads"),
        P("seq", "heads"),
        P("heads"),
        P("heads"),
        P("seq", "heads"),
        P("seq", "heads"),
        P("seq", "heads"),
        P("seq"),
    )
    return jax.shard_map(
        body,
        mesh=mesh,
        in_specs=placed,
        out_specs=(P("seq", "heads"), P("seq", "heads")),
        check_vma=False,
    )
```

profile of v0, /device:TPU:230, one launch (start us, length us, event | category | flops | bytes accessed | tf_op | source)
XLA Modules:
  0.0 448.4 jit_solution(15058796765951390284)
XLA Ops:
  18.8 69.7 %all-reduce.2 = (f32[32]{0:T(128)S(1)}, f32[256]{0:T(256)S(1)}) all-reduce(f32[32]{0:T(128)S(1)} %get-tuple-element.258, f32[256]{0:T(256)S(1)} %get-tuple-element.260), channel_id=2, replica_groups=mesh['seq'=32,'heads'=8] {'seq'}, use_global_device_ids=true, to_apply=%add | all-reduce | flops 288 | bytes 2304
  90.2 43.2 %all-gather.3 = s32[32,1,256]{2,1,0:T(1,128)S(1)} all-gather(s32[1,1,256]{2,1,0:T(1,128)} %bitcast.157), channel_id=1, replica_groups=mesh['seq'=32,'heads'=8] {'seq'}, dimensions={0}, use_global_device_ids=true | all-gather | bytes 33792 | tf_op jit(solution)/shard_map/all_gather | solution.py:160
  133.8 29.7 %all-gather.10.cloned.1.call-done = bf16[8192,128]{1,0:T(8,128)(2,1)} async-done(((bf16[256,128]{1,0:T(8,128)(2,1)}), bf16[8192,128]{1,0:T(8,128)(2,1)}) %all-gather.10.cloned.1.call-update) | async-done | bytes 2097168 | tf_op jit(solution)/shard_map/all_gather | solution.py:159
  163.5 139.9 %while.36 = (s32[]{:T(128)}, f32[8,256]{1,0:T(8,128)S(1)}, f32[8,256]{1,0:T(8,128)S(1)}, f32[8,256,128]{2,1,0:T(8,128)S(1)}, s32[8]{0:T(128)S(1)}, /*index=5*/s3...) while((s32[]{:T(128)}, f32[8,256]{1,0:T(8,128)S(1)}, ...), condition=%wide.region_7.8_spmd.clone, body=%wide.region_4.7_spmd.clone.sunk | while | flops 1098394880 | bytes 63070416 | solution.py:190
  165.9 5.6 %fusion.80 = (f32[8,256]{1,0:T(8,128)S(1)}, f32[1024,256,8]{1,0,2:T(8,128)}) fusion(pred[256,1024]{0,1:T(8,128)(4,1)S(1)} %compare_and_fusion.2, bf16[256,1,8,128]{3,0,2,1:T(8,128)(2,1)S(1)} %get-tuple-element.452, bf16[8,1024,1,128]{3,1,2,0:T(8,128)(2,1)} %get-tuple-element.451, s32[]{:T(128)} %get-tuple-element.430), kind=kOutput, calls=%fused_computation.8.clone.1 | convolution fusion | flops 543160320 | bytes 9445888 | tf_op jit(solution)/shard_map/while/body/eval_jaxpr/tgjd,sgd->gjts/dot_general | solution.py:69
  171.5 5.2 %fusion.81 = f32[8,256]{1,0:T(8,128)S(1)} fusion(f32[1024,256,8]{1,0,2:T(8,128)} %get-tuple-element.380, f32[8,256]{1,0:T(8,128)S(1)} %select_maximum_fusion.2, pred[256,1024]{0,1:T(8,128)(4,1)S(1)} %compare_and_fusion.2), kind=kLoop, calls=%fused_computation.11.clone.1 | loop fusion | flops 8386560 | bytes 8667136 | tf_op jit(solution)/shard_map/while/body/eval_jaxpr/reduce_sum | solution.py:79
  183.2 5.6 %fusion.80 = (f32[8,256]{1,0:T(8,128)S(1)}, f32[1024,256,8]{1,0,2:T(8,128)}) fusion(pred[256,1024]{0,1:T(8,128)(4,1)S(1)} %compare_and_fusion.2, bf16[256,1,8,128]{3,0,2,1:T(8,128)(2,1)S(1)} %get-tuple-element.452, bf16[8,1024,1,128]{3,1,2,0:T(8,128)(2,1)} %get-tuple-element.451, s32[]{:T(128)} %get-tuple-element.430), kind=kOutput, calls=%fused_computation.8.clone.1 | convolution fusion | flops 543160320 | bytes 9445888 | tf_op jit(solution)/shard_map/while/body/eval_jaxpr/tgjd,sgd->gjts/dot_general | solution.py:69
  188.8 5.3 %fusion.81 = f32[8,256]{1,0:T(8,128)S(1)} fusion(f32[1024,256,8]{1,0,2:T(8,128)} %get-tuple-element.380, f32[8,256]{1,0:T(8,128)S(1)} %select_maximum_fusion.2, pred[256,1024]{0,1:T(8,128)(4,1)S(1)} %compare_and_fusion.2), kind=kLoop, calls=%fused_computation.11.clone.1 | loop fusion | flops 8386560 | bytes 8667136 | tf_op jit(solution)/shard_map/while/body/eval_jaxpr/reduce_sum | solution.py:79
  194.8 3.4 fusion.83
  200.7 5.6 %fusion.80 = (f32[8,256]{1,0:T(8,128)S(1)}, f32[1024,256,8]{1,0,2:T(8,128)}) fusion(pred[256,1024]{0,1:T(8,128)(4,1)S(1)} %compare_and_fusion.2, bf16[256,1,8,128]{3,0,2,1:T(8,128)(2,1)S(1)} %get-tuple-element.452, bf16[8,1024,1,128]{3,1,2,0:T(8,128)(2,1)} %get-tuple-element.451, s32[]{:T(128)} %get-tuple-element.430), kind=kOutput, calls=%fused_computation.8.clone.1 | convolution fusion | flops 543160320 | bytes 9445888 | tf_op jit(solution)/shard_map/while/body/eval_jaxpr/tgjd,sgd->gjts/dot_general | solution.py:69
  206.3 5.2 %fusion.81 = f32[8,256]{1,0:T(8,128)S(1)} fusion(f32[1024,256,8]{1,0,2:T(8,128)} %get-tuple-element.380, f32[8,256]{1,0:T(8,128)S(1)} %select_maximum_fusion.2, pred[256,1024]{0,1:T(8,128)(4,1)S(1)} %compare_and_fusion.2), kind=kLoop, calls=%fused_computation.11.clone.1 | loop fusion | flops 8386560 | bytes 8667136 | tf_op jit(solution)/shard_map/while/body/eval_jaxpr/reduce_sum | solution.py:79
  218.0 6.0 %fusion.80 = (f32[8,256]{1,0:T(8,128)S(1)}, f32[1024,256,8]{1,0,2:T(8,128)}) fusion(pred[256,1024]{0,1:T(8,128)(4,1)S(1)} %compare_and_fusion.2, bf16[256,1,8,128]{3,0,2,1:T(8,128)(2,1)S(1)} %get-tuple-element.452, bf16[8,1024,1,128]{3,1,2,0:T(8,128)(2,1)} %get-tuple-element.451, s32[]{:T(128)} %get-tuple-element.430), kind=kOutput, calls=%fused_computation.8.clone.1 | convolution fusion | flops 543160320 | bytes 9445888 | tf_op jit(solution)/shard_map/while/body/eval_jaxpr/tgjd,sgd->gjts/dot_general | solution.py:69
  223.9 5.3 %fusion.81 = f32[8,256]{1,0:T(8,128)S(1)} fusion(f32[1024,256,8]{1,0,2:T(8,128)} %get-tuple-element.380, f32[8,256]{1,0:T(8,128)S(1)} %select_maximum_fusion.2, pred[256,1024]{0,1:T(8,128)(4,1)S(1)} %compare_and_fusion.2), kind=kLoop, calls=%fused_computation.11.clone.1 | loop fusion | flops 8386560 | bytes 8667136 | tf_op jit(solution)/shard_map/while/body/eval_jaxpr/reduce_sum | solution.py:79
  229.9 3.5 fusion.83
  235.8 5.6 %fusion.80 = (f32[8,256]{1,0:T(8,128)S(1)}, f32[1024,256,8]{1,0,2:T(8,128)}) fusion(pred[256,1024]{0,1:T(8,128)(4,1)S(1)} %compare_and_fusion.2, bf16[256,1,8,128]{3,0,2,1:T(8,128)(2,1)S(1)} %get-tuple-element.452, bf16[8,1024,1,128]{3,1,2,0:T(8,128)(2,1)} %get-tuple-element.451, s32[]{:T(128)} %get-tuple-element.430), kind=kOutput, calls=%fused_computation.8.clone.1 | convolution fusion | flops 543160320 | bytes 9445888 | tf_op jit(solution)/shard_map/while/body/eval_jaxpr/tgjd,sgd->gjts/dot_general | solution.py:69
  241.4 5.3 %fusion.81 = f32[8,256]{1,0:T(8,128)S(1)} fusion(f32[1024,256,8]{1,0,2:T(8,128)} %get-tuple-element.380, f32[8,256]{1,0:T(8,128)S(1)} %select_maximum_fusion.2, pred[256,1024]{0,1:T(8,128)(4,1)S(1)} %compare_and_fusion.2), kind=kLoop, calls=%fused_computation.11.clone.1 | loop fusion | flops 8386560 | bytes 8667136 | tf_op jit(solution)/shard_map/while/body/eval_jaxpr/reduce_sum | solution.py:79
  253.6 5.6 %fusion.80 = (f32[8,256]{1,0:T(8,128)S(1)}, f32[1024,256,8]{1,0,2:T(8,128)}) fusion(pred[256,1024]{0,1:T(8,128)(4,1)S(1)} %compare_and_fusion.2, bf16[256,1,8,128]{3,0,2,1:T(8,128)(2,1)S(1)} %get-tuple-element.452, bf16[8,1024,1,128]{3,1,2,0:T(8,128)(2,1)} %get-tuple-element.451, s32[]{:T(128)} %get-tuple-element.430), kind=kOutput, calls=%fused_computation.8.clone.1 | convolution fusion | flops 543160320 | bytes 9445888 | tf_op jit(solution)/shard_map/while/body/eval_jaxpr/tgjd,sgd->gjts/dot_general | solution.py:69
  259.2 5.2 %fusion.81 = f32[8,256]{1,0:T(8,128)S(1)} fusion(f32[1024,256,8]{1,0,2:T(8,128)} %get-tuple-element.380, f32[8,256]{1,0:T(8,128)S(1)} %select_maximum_fusion.2, pred[256,1024]{0,1:T(8,128)(4,1)S(1)} %compare_and_fusion.2), kind=kLoop, calls=%fused_computation.11.clone.1 | loop fusion | flops 8386560 | bytes 8667136 | tf_op jit(solution)/shard_map/while/body/eval_jaxpr/reduce_sum | solution.py:79
  271.1 5.6 %fusion.80 = (f32[8,256]{1,0:T(8,128)S(1)}, f32[1024,256,8]{1,0,2:T(8,128)}) fusion(pred[256,1024]{0,1:T(8,128)(4,1)S(1)} %compare_and_fusion.2, bf16[256,1,8,128]{3,0,2,1:T(8,128)(2,1)S(1)} %get-tuple-element.452, bf16[8,1024,1,128]{3,1,2,0:T(8,128)(2,1)} %get-tuple-element.451, s32[]{:T(128)} %get-tuple-element.430), kind=kOutput, calls=%fused_computation.8.clone.1 | convolution fusion | flops 543160320 | bytes 9445888 | tf_op jit(solution)/shard_map/while/body/eval_jaxpr/tgjd,sgd->gjts/dot_general | solution.py:69
  276.7 5.3 %fusion.81 = f32[8,256]{1,0:T(8,128)S(1)} fusion(f32[1024,256,8]{1,0,2:T(8,128)} %get-tuple-element.380, f32[8,256]{1,0:T(8,128)S(1)} %select_maximum_fusion.2, pred[256,1024]{0,1:T(8,128)(4,1)S(1)} %compare_and_fusion.2), kind=kLoop, calls=%fused_computation.11.clone.1 | loop fusion | flops 8386560 | bytes 8667136 | tf_op jit(solution)/shard_map/while/body/eval_jaxpr/reduce_sum | solution.py:79
  288.5 5.6 %fusion.80 = (f32[8,256]{1,0:T(8,128)S(1)}, f32[1024,256,8]{1,0,2:T(8,128)}) fusion(pred[256,1024]{0,1:T(8,128)(4,1)S(1)} %compare_and_fusion.2, bf16[256,1,8,128]{3,0,2,1:T(8,128)(2,1)S(1)} %get-tuple-element.452, bf16[8,1024,1,128]{3,1,2,0:T(8,128)(2,1)} %get-tuple-element.451, s32[]{:T(128)} %get-tuple-element.430), kind=kOutput, calls=%fused_computation.8.clone.1 | convolution fusion | flops 543160320 | bytes 9445888 | tf_op jit(solution)/shard_map/while/body/eval_jaxpr/tgjd,sgd->gjts/dot_general | solution.py:69
  294.1 5.2 %fusion.81 = f32[8,256]{1,0:T(8,128)S(1)} fusion(f32[1024,256,8]{1,0,2:T(8,128)} %get-tuple-element.380, f32[8,256]{1,0:T(8,128)S(1)} %select_maximum_fusion.2, pred[256,1024]{0,1:T(8,128)(4,1)S(1)} %compare_and_fusion.2), kind=kLoop, calls=%fused_computation.11.clone.1 | loop fusion | flops 8386560 | bytes 8667136 | tf_op jit(solution)/shard_map/while/body/eval_jaxpr/reduce_sum | solution.py:79
  304.6 117.0 %while.10 = (s32[]{:T(128)}, f32[8,128,128]{2,1,0:T(8,128)S(1)}, f32[1]{0:T(128)}, s32[]{:T(128)}, f32[32,1]{0,1:T(1,128)S(1)}, /*index=5*/f32[32,8]{1,0:T(8,128...) while((s32[]{:T(128)}, f32[8,128,128]{2,1,0:T(8,128)S(1)}, ...), condition=%wide.region_1.2_spmd, body=%wide.region_0.1_spmd.sunk | while | flops 262161 | bytes 1573157 | solution.py:21
  427.4 13.4 %psum.7 = f32[256]{0:T(256)S(1)} all-reduce(f32[256]{0:T(256)S(1)} %get-tuple-element.262), channel_id=1, replica_groups=mesh['seq'=32,'heads'=8] {'heads'}, use_global_device_ids=true, to_apply=%region_3.4 | all-reduce | flops 256 | bytes 2048 | tf_op jit(solution)/shard_map/psum | solution.py:126
  (227 shorter events, 115.1 us)
Async XLA Ops:
  7.2 414.6 %copy-start = (bf16[256,1024]{1,0:T(8,128)(2,1)S(1)}, bf16[256,1024]{1,0:T(8,128)(2,1)}, u32[]{:S(2)}) copy-start(bf16[256,1024]{1,0:T(8,128)(2,1)} %param.13) | copy-start | bytes 1572868
  7.2 126.6 %all-gather.8.cloned.1.call-start = ((), (), s32[]{:S(2)}) async-start(), calls=%async_computation | async-start | bytes 2162688 | tf_op jit(solution)/shard_map/all_gather | solution.py:158
  7.9 155.6 %all-gather.10.cloned.1.call-start = ((), (), s32[]{:S(2)}) async-start(), calls=%async_computation.1 | async-start | bytes 2162688 | tf_op jit(solution)/shard_map/all_gather | solution.py:159
  8.7 295.9 %all-gather.12.cloned.1.call-start = ((), (), s32[]{:S(2)}) async-start(), calls=%async_computation.2 | async-start | bytes 17301504 | tf_op jit(solution)/shard_map/all_gather | solution.py:13
  171.5 5.8 %copy-start.1 = (f32[1024,256,8]{1,0,2:T(8,128)S(1)}, f32[1024,256,8]{1,0,2:T(8,128)}, u32[]{:S(2)}) copy-start(f32[1024,256,8]{1,0,2:T(8,128)} %get-tuple-element.380) | copy-start | bytes 25165828 | tf_op jit(solution)/shard_map/while
  188.8 6.0 %copy-start.1 = (f32[1024,256,8]{1,0,2:T(8,128)S(1)}, f32[1024,256,8]{1,0,2:T(8,128)}, u32[]{:S(2)}) copy-start(f32[1024,256,8]{1,0,2:T(8,128)} %get-tuple-element.380) | copy-start | bytes 25165828 | tf_op jit(solution)/shard_map/while
  206.3 5.8 %copy-start.1 = (f32[1024,256,8]{1,0,2:T(8,128)S(1)}, f32[1024,256,8]{1,0,2:T(8,128)}, u32[]{:S(2)}) copy-start(f32[1024,256,8]{1,0,2:T(8,128)} %get-tuple-element.380) | copy-start | bytes 25165828 | tf_op jit(solution)/shard_map/while
  223.9 5.9 %copy-start.1 = (f32[1024,256,8]{1,0,2:T(8,128)S(1)}, f32[1024,256,8]{1,0,2:T(8,128)}, u32[]{:S(2)}) copy-start(f32[1024,256,8]{1,0,2:T(8,128)} %get-tuple-element.380) | copy-start | bytes 25165828 | tf_op jit(solution)/shard_map/while
  241.4 6.3 %copy-start.1 = (f32[1024,256,8]{1,0,2:T(8,128)S(1)}, f32[1024,256,8]{1,0,2:T(8,128)}, u32[]{:S(2)}) copy-start(f32[1024,256,8]{1,0,2:T(8,128)} %get-tuple-element.380) | copy-start | bytes 25165828 | tf_op jit(solution)/shard_map/while
  259.2 6.0 %copy-start.1 = (f32[1024,256,8]{1,0,2:T(8,128)S(1)}, f32[1024,256,8]{1,0,2:T(8,128)}, u32[]{:S(2)}) copy-start(f32[1024,256,8]{1,0,2:T(8,128)} %get-tuple-element.380) | copy-start | bytes 25165828 | tf_op jit(solution)/shard_map/while
  276.7 5.9 %copy-start.1 = (f32[1024,256,8]{1,0,2:T(8,128)S(1)}, f32[1024,256,8]{1,0,2:T(8,128)}, u32[]{:S(2)}) copy-start(f32[1024,256,8]{1,0,2:T(8,128)} %get-tuple-element.380) | copy-start | bytes 25165828 | tf_op jit(solution)/shard_map/while
  294.1 5.8 %copy-start.1 = (f32[1024,256,8]{1,0,2:T(8,128)S(1)}, f32[1024,256,8]{1,0,2:T(8,128)}, u32[]{:S(2)}) copy-start(f32[1024,256,8]{1,0,2:T(8,128)} %get-tuple-element.380) | copy-start | bytes 25165828 | tf_op jit(solution)/shard_map/while
  303.4 118.3 %copy-start.2 = (s32[256]{0:T(256)S(1)}, s32[256]{0:T(256)}, u32[]{:S(2)}) copy-start(s32[256]{0:T(256)} %get-tuple-element.465) | copy-start | bytes 3076
  304.6 136.3 %copy-start.3 = (f32[1024]{0:T(1024)S(1)}, f32[1024]{0:T(1024)}, u32[]{:S(2)}) copy-start(f32[1024]{0:T(1024)} %param.17) | copy-start | bytes 12292
Sparse Core Ops, SparseCore 0:
  10.6 75.2 all-gather.7
  88.5 74.9 all-gather.9
  166.6 137.0 all-gather.11
where the time goes:
time: 452 us; the launch traced here: 448 us
  blocking collectives  126 us (28%)
  other arithmetic  93.2 us (21%)
  matrix products  80.3 us (18%)
  loops' own time  67.7 us (15%)
  local copies, waits for them, and re-layouts  34.4 us (8%)
  waiting for transfers between devices  31.1 us (7%)
  between operations  15.2 us (3%)
    unnamed x1, blocking collectives  69.7 us
    another operation x1, loops' own time, carried_in(): return lax.fori_loop(0, place, carried_one, state)  61.6 us
    dot_general x8, matrix products, block_update(): jnp.einsum('tgjd,sgd->gjts', queries, k_blk, preferred_element_type=jnp.f...  45.2 us
    all_gather x1, blocking collectives, body(): seg_keys = lax.all_gather(segment_ids, 'seq', axis=0, tiled=True)  43.2 us
    reduce_sum x8, other arithmetic, block_update(): den = den * corr + jnp.sum(p, axis=2)  42.1 us
    add x31, other arithmetic, combine_states(): factor[:, None, None] * state_e + state_l  36.9 us
    all_gather x1, waiting for transfers between devices, body(): values = lax.all_gather(soft_v, 'seq', axis=0, tiled=True)  29.7 us
    dot_general x8, matrix products, block_update(): jnp.einsum('gjts,sgd->gjtd', weights, v_blk, preferred_element_type=jnp.f...  27.6 us
  transfers between devices with their start and end apart: 3, of which 1 were waited for; matrix products, arithmetic and copies ran while one was open for 31% of the time, Pallas kernels for 0%

commit v1 on v0

--- a/solution.py
+++ b/solution.py
@@ -157,7 +157,9 @@
     carry = start_carry
     keys = lax.all_gather(soft_k, "seq", axis=0, tiled=True)
     values = lax.all_gather(soft_v, "seq", axis=0, tiled=True)
-    seg_keys = lax.all_gather(segment_ids, "seq", axis=0, tiled=True)
+    seg_keys = jnp.concatenate(
+        lax.all_to_all(jnp.stack([segment_ids] * lax.axis_size("seq")), "seq", 0, 0), axis=0
+    )
     length = keys.shape[0]
     rows = math.gcd(length, 1024)
     count_blk = length // rows

time: 452 us -> 452 us (level)
  blocking collectives: 126 us -> 83.8 us
  waiting for transfers between devices: 31.1 us -> 64.8 us
  starting transfers between devices: 0.11 us -> 8.58 us
    all_gather x1 -> x0, blocking collectives: 43.2 us -> none  [body(): seg_keys = lax.all_gather(segment_ids, 'seq', axis=0, tiled=True)]
    all_gather x1, waiting for transfers between devices: 29.7 us -> 63.4 us  [body(): values = lax.all_gather(soft_v, 'seq', axis=0, tiled=True)]
    all_to_all x0 -> x1, starting transfers between devices: none -> 8.47 us  [body(): lax.all_to_all(jnp.stack([segment_ids] * lax.axis_size('seq')), 'seq', 0, 0)]
  transfers between devices with their start and end apart: 3 -> 4, of which waited for: 1 -> 1; matrix products, arithmetic and copies ran while one was open for 31% -> 32% of each run, Pallas kernels for 0% -> 0%
where the time goes in v1:
time: 452 us; the launch traced here: 449 us
  other arithmetic  93.2 us (21%)
  blocking collectives  83.8 us (19%)
  matrix products  80.5 us (18%)
  loops' own time  67.4 us (15%)
  waiting for transfers between devices  64.8 us (14%)
  local copies, waits for them, and re-layouts  35 us (8%)
  between operations  15.3 us (3%)
  starting transfers between devices  8.58 us (2%)
    unnamed x1, blocking collectives  69.6 us
    all_gather x1, waiting for transfers between devices, body(): values = lax.all_gather(soft_v, 'seq', axis=0, tiled=True)  63.4 us
    another operation x1, loops' own time, carried_in(): return lax.fori_loop(0, place, carried_one, state)  61.6 us
    dot_general x8, matrix products, block_update(): jnp.einsum('tgjd,sgd->gjts', queries, k_blk, preferred_element_type=jnp.f...  45.5 us
    reduce_sum x8, other arithmetic, block_update(): den = den * corr + jnp.sum(p, axis=2)  42.2 us
    add x31, other arithmetic, combine_states(): factor[:, None, None] * state_e + state_l  36.9 us
    dot_general x8, matrix products, block_update(): jnp.einsum('gjts,sgd->gjtd', weights, v_blk, preferred_element_type=jnp.f...  27.6 us
    dynamic_slice x31, local copies, waits for them, and re-layouts, carried_one(): lax.dynamic_index_in_dim(a, step, 0, False)  18.1 us
  transfers between devices with their start and end apart: 4, of which 1 were waited for; matrix products, arithmetic and copies ran while one was open for 32% of the time, Pallas kernels for 0%

profile of v1, /device:TPU:230, one launch (start us, length us, event | category | flops | bytes accessed | tf_op | source)
XLA Modules:
  0.0 448.5 jit_solution(7864581760835617507)
XLA Ops:
  20.1 8.5 %all-to-all-start = ((s32[32,1,256]{2,1,0:T(1,128)}), s32[32,1,256]{2,1,0:T(1,128)S(1)}, u32[]{:S(2)}, u32[]{:S(2)}) async-start(s32[32,1,256]{2,1,0:T(1,128)} %stack.2), calls=%async_computation | async-start | bytes 65536 | tf_op jit(solution)/shard_map/all_to_all | solution.py:161
  28.6 69.6 %all-reduce.2 = (f32[32]{0:T(128)S(1)}, f32[256]{0:T(256)S(1)}) all-reduce(f32[32]{0:T(128)S(1)} %get-tuple-element.258, f32[256]{0:T(256)S(1)} %get-tuple-element.260), channel_id=2, replica_groups=mesh['seq'=32,'heads'=8] {'seq'}, use_global_device_ids=true, to_apply=%add | all-reduce | flops 288 | bytes 2304
  100.2 63.4 %all-gather.9.cloned.1.call-done = bf16[8192,128]{1,0:T(8,128)(2,1)} async-done(((bf16[256,128]{1,0:T(8,128)(2,1)}), bf16[8192,128]{1,0:T(8,128)(2,1)}) %all-gather.9.cloned.1.call-update) | async-done | bytes 2097168 | tf_op jit(solution)/shard_map/all_gather | solution.py:159
  163.7 139.1 %while.36 = (s32[]{:T(128)}, f32[8,256]{1,0:T(8,128)S(1)}, f32[8,256]{1,0:T(8,128)S(1)}, f32[8,256,128]{2,1,0:T(8,128)S(1)}, s32[8]{0:T(128)S(1)}, /*index=5*/s3...) while((s32[]{:T(128)}, f32[8,256]{1,0:T(8,128)S(1)}, ...), condition=%wide.region_7.8_spmd.clone, body=%wide.region_4.7_spmd.clone.sunk | while | flops 1098394880 | bytes 63070416 | solution.py:192
  166.0 5.6 %fusion.80 = (f32[8,256]{1,0:T(8,128)S(1)}, f32[1024,256,8]{1,0,2:T(8,128)}) fusion(pred[256,1024]{0,1:T(8,128)(4,1)S(1)} %compare_and_fusion.2, bf16[256,1,8,128]{3,0,2,1:T(8,128)(2,1)S(1)} %get-tuple-element.452, bf16[8,1024,1,128]{3,1,2,0:T(8,128)(2,1)} %get-tuple-element.451, s32[]{:T(128)} %get-tuple-element.430), kind=kOutput, calls=%fused_computation.8.clone.1 | convolution fusion | flops 543160320 | bytes 9445888 | tf_op jit(solution)/shard_map/while/body/eval_jaxpr/tgjd,sgd->gjts/dot_general | solution.py:69
  171.6 5.2 %fusion.81 = f32[8,256]{1,0:T(8,128)S(1)} fusion(f32[1024,256,8]{1,0,2:T(8,128)} %get-tuple-element.380, f32[8,256]{1,0:T(8,128)S(1)} %select_maximum_fusion.2, pred[256,1024]{0,1:T(8,128)(4,1)S(1)} %compare_and_fusion.2), kind=kLoop, calls=%fused_computation.11.clone.1 | loop fusion | flops 8386560 | bytes 8667136 | tf_op jit(solution)/shard_map/while/body/eval_jaxpr/reduce_sum | solution.py:79
  183.1 5.6 %fusion.80 = (f32[8,256]{1,0:T(8,128)S(1)}, f32[1024,256,8]{1,0,2:T(8,128)}) fusion(pred[256,1024]{0,1:T(8,128)(4,1)S(1)} %compare_and_fusion.2, bf16[256,1,8,128]{3,0,2,1:T(8,128)(2,1)S(1)} %get-tuple-element.452, bf16[8,1024,1,128]{3,1,2,0:T(8,128)(2,1)} %get-tuple-element.451, s32[]{:T(128)} %get-tuple-element.430), kind=kOutput, calls=%fused_computation.8.clone.1 | convolution fusion | flops 543160320 | bytes 9445888 | tf_op jit(solution)/shard_map/while/body/eval_jaxpr/tgjd,sgd->gjts/dot_general | solution.py:69
  188.7 5.3 %fusion.81 = f32[8,256]{1,0:T(8,128)S(1)} fusion(f32[1024,256,8]{1,0,2:T(8,128)} %get-tuple-element.380, f32[8,256]{1,0:T(8,128)S(1)} %select_maximum_fusion.2, pred[256,1024]{0,1:T(8,128)(4,1)S(1)} %compare_and_fusion.2), kind=kLoop, calls=%fused_computation.11.clone.1 | loop fusion | flops 8386560 | bytes 8667136 | tf_op jit(solution)/shard_map/while/body/eval_jaxpr/reduce_sum | solution.py:79
  200.5 5.6 %fusion.80 = (f32[8,256]{1,0:T(8,128)S(1)}, f32[1024,256,8]{1,0,2:T(8,128)}) fusion(pred[256,1024]{0,1:T(8,128)(4,1)S(1)} %compare_and_fusion.2, bf16[256,1,8,128]{3,0,2,1:T(8,128)(2,1)S(1)} %get-tuple-element.452, bf16[8,1024,1,128]{3,1,2,0:T(8,128)(2,1)} %get-tuple-element.451, s32[]{:T(128)} %get-tuple-element.430), kind=kOutput, calls=%fused_computation.8.clone.1 | convolution fusion | flops 543160320 | bytes 9445888 | tf_op jit(solution)/shard_map/while/body/eval_jaxpr/tgjd,sgd->gjts/dot_general | solution.py:69
  206.1 5.2 %fusion.81 = f32[8,256]{1,0:T(8,128)S(1)} fusion(f32[1024,256,8]{1,0,2:T(8,128)} %get-tuple-element.380, f32[8,256]{1,0:T(8,128)S(1)} %select_maximum_fusion.2, pred[256,1024]{0,1:T(8,128)(4,1)S(1)} %compare_and_fusion.2), kind=kLoop, calls=%fused_computation.11.clone.1 | loop fusion | flops 8386560 | bytes 8667136 | tf_op jit(solution)/shard_map/while/body/eval_jaxpr/reduce_sum | solution.py:79
  217.6 6.2 %fusion.80 = (f32[8,256]{1,0:T(8,128)S(1)}, f32[1024,256,8]{1,0,2:T(8,128)}) fusion(pred[256,1024]{0,1:T(8,128)(4,1)S(1)} %compare_and_fusion.2, bf16[256,1,8,128]{3,0,2,1:T(8,128)(2,1)S(1)} %get-tuple-element.452, bf16[8,1024,1,128]{3,1,2,0:T(8,128)(2,1)} %get-tuple-element.451, s32[]{:T(128)} %get-tuple-element.430), kind=kOutput, calls=%fused_computation.8.clone.1 | convolution fusion | flops 543160320 | bytes 9445888 | tf_op jit(solution)/shard_map/while/body/eval_jaxpr/tgjd,sgd->gjts/dot_general | solution.py:69
  223.9 5.3 %fusion.81 = f32[8,256]{1,0:T(8,128)S(1)} fusion(f32[1024,256,8]{1,0,2:T(8,128)} %get-tuple-element.380, f32[8,256]{1,0:T(8,128)S(1)} %select_maximum_fusion.2, pred[256,1024]{0,1:T(8,128)(4,1)S(1)} %compare_and_fusion.2), kind=kLoop, calls=%fused_computation.11.clone.1 | loop fusion | flops 8386560 | bytes 8667136 | tf_op jit(solution)/shard_map/while/body/eval_jaxpr/reduce_sum | solution.py:79
  229.8 3.5 fusion.83
  235.6 5.6 %fusion.80 = (f32[8,256]{1,0:T(8,128)S(1)}, f32[1024,256,8]{1,0,2:T(8,128)}) fusion(pred[256,1024]{0,1:T(8,128)(4,1)S(1)} %compare_and_fusion.2, bf16[256,1,8,128]{3,0,2,1:T(8,128)(2,1)S(1)} %get-tuple-element.452, bf16[8,1024,1,128]{3,1,2,0:T(8,128)(2,1)} %get-tuple-element.451, s32[]{:T(128)} %get-tuple-element.430), kind=kOutput, calls=%fused_computation.8.clone.1 | convolution fusion | flops 543160320 | bytes 9445888 | tf_op jit(solution)/shard_map/while/body/eval_jaxpr/tgjd,sgd->gjts/dot_general | solution.py:69
  241.2 5.3 %fusion.81 = f32[8,256]{1,0:T(8,128)S(1)} fusion(f32[1024,256,8]{1,0,2:T(8,128)} %get-tuple-element.380, f32[8,256]{1,0:T(8,128)S(1)} %select_maximum_fusion.2, pred[256,1024]{0,1:T(8,128)(4,1)S(1)} %compare_and_fusion.2), kind=kLoop, calls=%fused_computation.11.clone.1 | loop fusion | flops 8386560 | bytes 8667136 | tf_op jit(solution)/shard_map/while/body/eval_jaxpr/reduce_sum | solution.py:79
  247.4 3.4 fusion.83
  253.2 5.6 %fusion.80 = (f32[8,256]{1,0:T(8,128)S(1)}, f32[1024,256,8]{1,0,2:T(8,128)}) fusion(pred[256,1024]{0,1:T(8,128)(4,1)S(1)} %compare_and_fusion.2, bf16[256,1,8,128]{3,0,2,1:T(8,128)(2,1)S(1)} %get-tuple-element.452, bf16[8,1024,1,128]{3,1,2,0:T(8,128)(2,1)} %get-tuple-element.451, s32[]{:T(128)} %get-tuple-element.430), kind=kOutput, calls=%fused_computation.8.clone.1 | convolution fusion | flops 543160320 | bytes 9445888 | tf_op jit(solution)/shard_map/while/body/eval_jaxpr/tgjd,sgd->gjts/dot_general | solution.py:69
  258.8 5.2 %fusion.81 = f32[8,256]{1,0:T(8,128)S(1)} fusion(f32[1024,256,8]{1,0,2:T(8,128)} %get-tuple-element.380, f32[8,256]{1,0:T(8,128)S(1)} %select_maximum_fusion.2, pred[256,1024]{0,1:T(8,128)(4,1)S(1)} %compare_and_fusion.2), kind=kLoop, calls=%fused_computation.11.clone.1 | loop fusion | flops 8386560 | bytes 8667136 | tf_op jit(solution)/shard_map/while/body/eval_jaxpr/reduce_sum | solution.py:79
  270.6 5.6 %fusion.80 = (f32[8,256]{1,0:T(8,128)S(1)}, f32[1024,256,8]{1,0,2:T(8,128)}) fusion(pred[256,1024]{0,1:T(8,128)(4,1)S(1)} %compare_and_fusion.2, bf16[256,1,8,128]{3,0,2,1:T(8,128)(2,1)S(1)} %get-tuple-element.452, bf16[8,1024,1,128]{3,1,2,0:T(8,128)(2,1)} %get-tuple-element.451, s32[]{:T(128)} %get-tuple-element.430), kind=kOutput, calls=%fused_computation.8.clone.1 | convolution fusion | flops 543160320 | bytes 9445888 | tf_op jit(solution)/shard_map/while/body/eval_jaxpr/tgjd,sgd->gjts/dot_general | solution.py:69
  276.2 5.3 %fusion.81 = f32[8,256]{1,0:T(8,128)S(1)} fusion(f32[1024,256,8]{1,0,2:T(8,128)} %get-tuple-element.380, f32[8,256]{1,0:T(8,128)S(1)} %select_maximum_fusion.2, pred[256,1024]{0,1:T(8,128)(4,1)S(1)} %compare_and_fusion.2), kind=kLoop, calls=%fused_computation.11.clone.1 | loop fusion | flops 8386560 | bytes 8667136 | tf_op jit(solution)/shard_map/while/body/eval_jaxpr/reduce_sum | solution.py:79
  287.9 5.6 %fusion.80 = (f32[8,256]{1,0:T(8,128)S(1)}, f32[1024,256,8]{1,0,2:T(8,128)}) fusion(pred[256,1024]{0,1:T(8,128)(4,1)S(1)} %compare_and_fusion.2, bf16[256,1,8,128]{3,0,2,1:T(8,128)(2,1)S(1)} %get-tuple-element.452, bf16[8,1024,1,128]{3,1,2,0:T(8,128)(2,1)} %get-tuple-element.451, s32[]{:T(128)} %get-tuple-element.430), kind=kOutput, calls=%fused_computation.8.clone.1 | convolution fusion | flops 543160320 | bytes 9445888 | tf_op jit(solution)/shard_map/while/body/eval_jaxpr/tgjd,sgd->gjts/dot_general | solution.py:69
  293.5 5.2 %fusion.81 = f32[8,256]{1,0:T(8,128)S(1)} fusion(f32[1024,256,8]{1,0,2:T(8,128)} %get-tuple-element.380, f32[8,256]{1,0:T(8,128)S(1)} %select_maximum_fusion.2, pred[256,1024]{0,1:T(8,128)(4,1)S(1)} %compare_and_fusion.2), kind=kLoop, calls=%fused_computation.11.clone.1 | loop fusion | flops 8386560 | bytes 8667136 | tf_op jit(solution)/shard_map/while/body/eval_jaxpr/reduce_sum | solution.py:79
  304.0 117.0 %while.10 = (s32[]{:T(128)}, f32[8,128,128]{2,1,0:T(8,128)S(1)}, f32[1]{0:T(128)}, s32[]{:T(128)}, f32[32,1]{0,1:T(1,128)S(1)}, /*index=5*/f32[32,8]{1,0:T(8,128...) while((s32[]{:T(128)}, f32[8,128,128]{2,1,0:T(8,128)S(1)}, ...), condition=%wide.region_1.2_spmd, body=%wide.region_0.1_spmd.sunk | while | flops 262161 | bytes 1573157 | solution.py:21
  426.8 14.2 %psum.7 = f32[256]{0:T(256)S(1)} all-reduce(f32[256]{0:T(256)S(1)} %get-tuple-element.262), channel_id=1, replica_groups=mesh['seq'=32,'heads'=8] {'heads'}, use_global_device_ids=true, to_apply=%region_3.4 | all-reduce | flops 256 | bytes 2048 | tf_op jit(solution)/shard_map/psum | solution.py:126
  (229 shorter events, 115.7 us)
Async XLA Ops:
  7.2 414.0 %copy-start = (bf16[256,1024]{1,0:T(8,128)(2,1)S(1)}, bf16[256,1024]{1,0:T(8,128)(2,1)}, u32[]{:S(2)}) copy-start(bf16[256,1024]{1,0:T(8,128)(2,1)} %param.13) | copy-start | bytes 1572868
  7.2 93.1 %all-gather.7.cloned.1.call-start = ((), (), s32[]{:S(2)}) async-start(), calls=%async_computation.1 | async-start | bytes 2162688 | tf_op jit(solution)/shard_map/all_gather | solution.py:158
  7.9 155.7 %all-gather.9.cloned.1.call-start = ((), (), s32[]{:S(2)}) async-start(), calls=%async_computation.2 | async-start | bytes 2162688 | tf_op jit(solution)/shard_map/all_gather | solution.py:159
  8.7 295.3 %all-gather.11.cloned.1.call-start = ((), (), s32[]{:S(2)}) async-start(), calls=%async_computation.3 | async-start | bytes 17301504 | tf_op jit(solution)/shard_map/all_gather | solution.py:13
  20.1 80.0 %all-to-all-start = ((s32[32,1,256]{2,1,0:T(1,128)}), s32[32,1,256]{2,1,0:T(1,128)S(1)}, u32[]{:S(2)}, u32[]{:S(2)}) async-start(s32[32,1,256]{2,1,0:T(1,128)} %stack.2), calls=%async_computation | async-start | bytes 65536 | tf_op jit(solution)/shard_map/all_to_all | solution.py:161
  171.6 5.8 %copy-start.1 = (f32[1024,256,8]{1,0,2:T(8,128)S(1)}, f32[1024,256,8]{1,0,2:T(8,128)}, u32[]{:S(2)}) copy-start(f32[1024,256,8]{1,0,2:T(8,128)} %get-tuple-element.380) | copy-start | bytes 25165828 | tf_op jit(solution)/shard_map/while
  188.7 6.0 %copy-start.1 = (f32[1024,256,8]{1,0,2:T(8,128)S(1)}, f32[1024,256,8]{1,0,2:T(8,128)}, u32[]{:S(2)}) copy-start(f32[1024,256,8]{1,0,2:T(8,128)} %get-tuple-element.380) | copy-start | bytes 25165828 | tf_op jit(solution)/shard_map/while
  206.1 5.8 %copy-start.1 = (f32[1024,256,8]{1,0,2:T(8,128)S(1)}, f32[1024,256,8]{1,0,2:T(8,128)}, u32[]{:S(2)}) copy-start(f32[1024,256,8]{1,0,2:T(8,128)} %get-tuple-element.380) | copy-start | bytes 25165828 | tf_op jit(solution)/shard_map/while
  223.9 5.9 %copy-start.1 = (f32[1024,256,8]{1,0,2:T(8,128)S(1)}, f32[1024,256,8]{1,0,2:T(8,128)}, u32[]{:S(2)}) copy-start(f32[1024,256,8]{1,0,2:T(8,128)} %get-tuple-element.380) | copy-start | bytes 25165828 | tf_op jit(solution)/shard_map/while
  241.2 6.2 %copy-start.1 = (f32[1024,256,8]{1,0,2:T(8,128)S(1)}, f32[1024,256,8]{1,0,2:T(8,128)}, u32[]{:S(2)}) copy-start(f32[1024,256,8]{1,0,2:T(8,128)} %get-tuple-element.380) | copy-start | bytes 25165828 | tf_op jit(solution)/shard_map/while
  258.8 6.0 %copy-start.1 = (f32[1024,256,8]{1,0,2:T(8,128)S(1)}, f32[1024,256,8]{1,0,2:T(8,128)}, u32[]{:S(2)}) copy-start(f32[1024,256,8]{1,0,2:T(8,128)} %get-tuple-element.380) | copy-start | bytes 25165828 | tf_op jit(solution)/shard_map/while
  276.2 5.9 %copy-start.1 = (f32[1024,256,8]{1,0,2:T(8,128)S(1)}, f32[1024,256,8]{1,0,2:T(8,128)}, u32[]{:S(2)}) copy-start(f32[1024,256,8]{1,0,2:T(8,128)} %get-tuple-element.380) | copy-start | bytes 25165828 | tf_op jit(solution)/shard_map/while
  293.5 5.8 %copy-start.1 = (f32[1024,256,8]{1,0,2:T(8,128)S(1)}, f32[1024,256,8]{1,0,2:T(8,128)}, u32[]{:S(2)}) copy-start(f32[1024,256,8]{1,0,2:T(8,128)} %get-tuple-element.380) | copy-start | bytes 25165828 | tf_op jit(solution)/shard_map/while
  302.8 118.3 %copy-start.2 = (s32[256]{0:T(256)S(1)}, s32[256]{0:T(256)}, u32[]{:S(2)}) copy-start(s32[256]{0:T(256)} %get-tuple-element.466) | copy-start | bytes 3076
  304.0 137.1 %copy-start.3 = (f32[1024]{0:T(1024)S(1)}, f32[1024]{0:T(1024)}, u32[]{:S(2)}) copy-start(f32[1024]{0:T(1024)} %param.17) | copy-start | bytes 12292
Sparse Core Ops, SparseCore 0:
  10.6 75.4 all-gather.6
  88.7 74.9 all-gather.8
  166.8 137.0 all-gather.10
